TPU v7x, 256 devices: a whole 4x4x8 slice. The times are simulated.
256 devices in a mesh: dp: 4 (over y), space: 64 (over x, z, core).
Axes of the slice: x: 4, y: 4, z: 8, core: 2. Of those that a mesh axis runs over, the one named last changes fastest.
Arguments:
- volume: bfloat16 [4, 128, 4, 64, 128], P('dp', 'space'), may hold values from -30 to 30
- weights_one: bfloat16 [3, 3, 3, 128, 256], replicated, may hold values from -0.109375 to 0.109375
- gain_one: float32 [256], replicated, may hold values from 0.1 to 1.9
- shift_one: float32 [256], replicated, may hold values from -3 to 3
- weights_two: bfloat16 [3, 3, 3, 8, 256], P(None, None, None, None, 'space'), may hold values from -0.4375 to 0.4375
- gain_two: float32 [256], P('space'), may hold values from 0.1 to 1.9
- shift_two: float32 [256], P('space'), may hold values from -3 to 3
- upstream: bfloat16 [4, 256, 64, 2, 32], P('dp', 'space'), may hold values from -6 to 6
Outputs:
- result: bfloat16 [4, 256, 64, 2, 32], P('dp', 'space')
- grad_weights_one: float32 [3, 3, 3, 128, 256], P(None, None, None, None, 'space')
- grad_weights_two: float32 [3, 3, 3, 8, 256], P(None, None, None, None, 'space')
All inputs are finite; a program needn't handle non-finite values.
Results may differ from a plain program's by a relative error of at most 0.0057.
Values may be sent and summed in bfloat16 or wider, within the bound.
A program may use at most 64 MiB of HBM per device.

v0:
```python
import math
import jax
import jax.numpy as jnp
from jax import lax
from jax.sharding import PartitionSpec as P

EPS = 1e-05
LAST = ("NDHWC", "DHWIO", "NDHWC")
FIRST = ("NCDHW", "DHWIO", "NCDHW")


def from_behind(value, axis, steps):
    count = lax.axis_size(axis)
    leading, last = (max(0, -steps), min(count, count - steps))
    return lax.ppermute(value, axis, [(source, source + steps) for source in range(leading, last)])


def combined_all(part, axis, combine):
    gathered = jax.tree.map(lambda a: lax.all_gather(a, axis), part)

    def take(source):
        return jax.tree.map(lambda a: lax.dynamic_index_in_dim(a, source, 0, False), gathered)

    return lax.fori_loop(
        1, lax.axis_size(axis), lambda source, state: combine(state, take(source)), take(0)
    )


def welford(left, right):
    count_a, mean_a, spread_a = left
    count_b, mean_b, spread_b = right
    merged = count_a + count_b
    delta = mean_b - mean_a
    return (
        merged,
        mean_a + delta * (count_b / merged),
        spread_a + spread_b + delta * delta * (count_a * count_b / merged),
    )


def group_filter(inputs, grads):
    return lax.conv_general_dilated(
        inputs,
        grads,
        (1, 1, 1),
        ((1, 1), (1, 1), (1, 1)),
        dimension_numbers=("CNDHW", "IODHW", "DHWNC"),
        preferred_element_type=jnp.float32,
    )


def per_device(
    volume, weights_one, gain_one, shift_one, weights_two, gain_two, shift_two, upstream
):
    planes = lax.axis_size("space")
    below = from_behind(volume[:, 1:], "space", 1)
    stacked = jnp.concatenate([below, volume], axis=1)
    pre_one = lax.conv_general_dilated(
        stacked,
        weights_one,
        (2, 2, 2),
        ((0, 0), (1, 1), (1, 1)),
        dimension_numbers=LAST,
        preferred_element_type=jnp.float32,
    )
    lead = pre_one.shape[0]
    count = float(lax.axis_size("dp") * lead * planes * pre_one.shape[2] * pre_one.shape[3])
    axes_last = (0, 1, 2, 3)
    mean_one = lax.psum(jnp.sum(pre_one, axis=axes_last), ("dp", "space")) / count
    spread_one = lax.psum(jnp.sum(jnp.square(pre_one - mean_one), axis=axes_last), ("dp", "space"))
    var_one = spread_one / count
    inv_one = lax.rsqrt(var_one + EPS)
    norm_one = (pre_one - mean_one) * inv_one
    act_in = norm_one * gain_one + shift_one
    activated = jax.nn.silu(act_in).astype(jnp.bfloat16)
    act_first = jnp.transpose(activated, (0, 4, 1, 2, 3))
    own_width = weights_two.shape[4]
    group_width = weights_two.shape[3]
    window = max(own_width, group_width)
    replicas = window // own_width
    channels = act_first.shape[1]
    tail = act_first.shape[2:]
    parts = act_first.reshape((lead, channels // window, 1, window) + tail)
    copies = jnp.broadcast_to(parts, (lead, channels // window, replicas, window) + tail)
    outgoing = copies.reshape((lead, planes * window) + tail)
    inputs = lax.all_to_all(outgoing, "space", split_axis=1, concat_axis=2, tiled=True)
    groups_here = window // group_width
    per_group = own_width // groups_here
    padding_one = ((1, 1), (1, 1), (1, 1))
    pre_two = lax.conv_general_dilated(
        inputs,
        weights_two,
        (1, 1, 1),
        padding_one,
        dimension_numbers=FIRST,
        feature_group_count=groups_here,
        preferred_element_type=jnp.float32,
    )
    axes_first = (0, 2, 3, 4)
    local_mean_two = jnp.mean(pre_two, axis=axes_first, keepdims=True)
    local_spread_two = jnp.sum(jnp.square(pre_two - local_mean_two), axis=axes_first, keepdims=True)
    local_count_two = float(pre_two.size // pre_two.shape[1])
    merged_two, mean_two, spread_two = combined_all(
        (jnp.full((1, 1, 1, 1, 1), local_count_two, jnp.float32), local_mean_two, local_spread_two),
        "dp",
        welford,
    )
    inv_two = lax.rsqrt(spread_two / merged_two + EPS)
    norm_two = (pre_two - mean_two) * inv_two
    gain_col = gain_two.reshape((1, -1, 1, 1, 1))
    shift_col = shift_two.reshape((1, -1, 1, 1, 1))
    result = (norm_two * gain_col + shift_col).astype(jnp.bfloat16)
    grad_norm_two = upstream.astype(jnp.float32) * gain_col * (1.0 / math.sqrt(count))
    first_sum, second_sum = lax.psum(
        (
            jnp.sum(grad_norm_two, axis=axes_first, keepdims=True),
            jnp.sum(grad_norm_two * norm_two, axis=axes_first, keepdims=True),
        ),
        "dp",
    )
    grad_pre_two = (
        inv_two * (grad_norm_two - first_sum / count - norm_two * (second_sum / count))
    ).astype(jnp.bfloat16)
    grouped_inputs = inputs.reshape((lead, groups_here, group_width) + inputs.shape[2:])
    grouped_grads = grad_pre_two.reshape((lead, groups_here, per_group) + grad_pre_two.shape[2:])
    pieces = jax.vmap(group_filter, in_axes=(1, 1))(grouped_inputs, grouped_grads)
    local_two = jnp.transpose(pieces, (1, 2, 3, 4, 0, 5)).reshape((3, 3, 3, group_width, own_width))
    grad_weights_two = lax.psum(local_two, "dp")
    flipped = weights_two[::-1, ::-1, ::-1]
    turned = (
        flipped.reshape((3, 3, 3, group_width, groups_here, per_group))
        .transpose((0, 1, 2, 5, 4, 3))
        .reshape((3, 3, 3, per_group, window))
    )
    partial_grad = lax.conv_general_dilated(
        grad_pre_two,
        turned,
        (1, 1, 1),
        padding_one,
        dimension_numbers=FIRST,
        feature_group_count=groups_here,
        preferred_element_type=jnp.float32,
    )
    arrived = lax.all_to_all(partial_grad, "space", split_axis=2, concat_axis=1, tiled=True)
    grad_act = jnp.sum(
        arrived.reshape((lead, channels // window, replicas, window) + arrived.shape[2:]), axis=2
    ).reshape((lead, channels) + arrived.shape[2:])
    grad_last = jnp.transpose(grad_act, (0, 2, 3, 4, 1))
    sigma = jax.nn.sigmoid(act_in)
    grad_norm_one = grad_last * (sigma * (1.0 + act_in * (1.0 - sigma))) * gain_one
    third_sum, fourth_sum = lax.psum(
        (jnp.sum(grad_norm_one, axis=axes_last), jnp.sum(grad_norm_one * norm_one, axis=axes_last)),
        ("dp", "space"),
    )
    grad_pre_one = (
        inv_one * (grad_norm_one - third_sum / count - norm_one * (fourth_sum / count))
    ).astype(jnp.bfloat16)
    local_one = lax.conv_general_dilated(
        stacked,
        grad_pre_one,
        (1, 1, 1),
        ((0, 0), (1, 0), (1, 0)),
        rhs_dilation=(2, 2, 2),
        dimension_numbers=("CDHWN", "IDHWO", "DHWNC"),
        preferred_element_type=jnp.float32,
    )
    summed = lax.psum(local_one, "dp")
    grad_weights_one = lax.psum_scatter(summed, "space", scatter_dimension=4, tiled=True)
    return (result, grad_weights_one, grad_weights_two)


def solution(mesh):
    return jax.shard_map(
        per_device,
        mesh=mesh,
        in_specs=(
            P("dp", "space", None, None, None),
            P(),
            P(),
            P(),
            P(None, None, None, None, "space"),
            P("space"),
            P("space"),
            P("dp", "space", None, None, None),
        ),
        out_specs=(
            P("dp", "space", None, None, None),
            P(None, None, None, None, "space"),
            P(None, None, None, None, "space"),
        ),
        check_vma=False,
    )
```

profile of v0, /device:TPU:2, one launch (start us, length us, event | category | flops | bytes accessed | tf_op | source)
XLA Modules:
  0.0 559.2 jit_solution(1003987523249396105)
XLA Ops:
  8.3 1.9 collective-permute-start
  10.2 7.9 %collective-permute-done = bf16[1,1,4,64,128]{4,0,3,2,1:T(2,128)(2,1)S(1)} collective-permute-done((bf16[1,1,4,64,128]{4,0,3,2,1:T(2,128)(2,1)S(1)}, bf16[1,1,4,64,128]{4,0,3,2,1:T(2,128)(2,1)S(1)}, u32[]{:S(2)}, u32[]{:S(2)}) %collective-permute-start) | collective-permute-done | bytes 65568 | tf_op jit(solution)/shard_map/ppermute | solution.py:15
  21.0 74.9 %psum.56 = f32[256]{0:T(256)S(1)} all-reduce(f32[256]{0:T(256)S(1)} %get-tuple-element.289), channel_id=1, replica_groups=mesh['dp'=4,'space'=64] {'dp','space'}, use_global_device_ids=true, to_apply=%region_1.0 | all-reduce | flops 256 | bytes 2048 | tf_op jit(solution)/shard_map/psum | solution.py:69
  95.9 74.4 %psum.57 = f32[256]{0:T(256)S(1)} all-reduce(f32[256]{0:T(256)S(1)} %select_reduce_fusion.2), channel_id=1, replica_groups=mesh['dp'=4,'space'=64] {'dp','space'}, use_global_device_ids=true, to_apply=%region_3.0 | all-reduce | flops 256 | bytes 2048 | tf_op jit(solution)/shard_map/psum | solution.py:70
  172.2 8.1 %all-to-all-start = ((bf16[64,2,256]{2,1,0:T(2,128)(2,1)}), bf16[64,2,256]{2,1,0:T(2,128)(2,1)S(1)}, u32[]{:S(2)}, u32[]{:S(2)}) async-start(bf16[64,2,256]{2,1,0:T(2,128)(2,1)} %reshape.180), calls=%async_computation | async-start | bytes 131072 | tf_op jit(solution)/shard_map/all_to_all | solution.py:86
  183.0 6.0 %all-to-all-done = bf16[64,2,256]{2,1,0:T(2,128)(2,1)S(1)} async-done(((bf16[64,2,256]{2,1,0:T(2,128)(2,1)}), bf16[64,2,256]{2,1,0:T(2,128)(2,1)S(1)}, u32[]{:S(2)}, u32[]{:S(2)}) %all-to-all-start) | async-done | bytes 65568 | tf_op jit(solution)/shard_map/all_to_all | solution.py:86
  190.2 2.1 copy.207
  192.5 5.6 fusion.8
  198.1 1.7 copy.208
  200.5 8.6 %all-reduce.7 = (f32[4]{0:T(128)S(1)}, f32[16]{0:T(128)S(1)}, f32[16]{0:T(128)S(1)}) all-reduce(f32[4]{0:T(128)S(1)} %dynamic-update-slice, f32[16]{0:T(128)S(1)} %get-tuple-element.288, f32[16]{0:T(128)S(1)} %dynamic-update-slice.2), channel_id=1, replica_groups=mesh['dp'=4,'space'=64] {'dp'}, use_global_device_ids=true, to_apply=%add | all-reduce | flops 36 | bytes 288
  209.8 13.6 %while.19 = (s32[]{:T(128)}, f32[1,1,1,1,1]{4,3,2,1,0:T(1,128)}, f32[1,4,1,1,1]{1,4,3,2,0:T(1,128)S(1)}, f32[1,4,1,1,1]{1,4,3,2,0:T(1,128)S(1)}, f32[4,1,1,1,1,1...) while((s32[]{:T(128)}, f32[1,1,1,1,1]{4,3,2,1,0:T(1,128)}, ...), condition=%wide.region_7.8_spmd, body=%wide.region_6.7_spmd.sunk | while | flops 37 | bytes 303 | solution.py:24
  225.2 9.4 %all-reduce.6 = (f32[1,4,1,1,1]{1,4,3,2,0:T(1,128)S(1)}, f32[1,4,1,1,1]{1,4,3,2,0:T(1,128)S(1)}) all-reduce(f32[1,4,1,1,1]{1,4,3,2,0:T(1,128)S(1)} %bitcast.177, f32[1,4,1,1,1]{1,4,3,2,0:T(1,128)S(1)} %bitcast.176), channel_id=1, replica_groups=mesh['dp'=4,'space'=64] {'dp'}, use_global_device_ids=true, to_apply=%region_11.12 | all-reduce | flops 8 | bytes 64 | tf_op jit(solution)/shard_map/psum | solution.py:114
  235.5 6.9 %convolution_select_fusion = f32[64,2,8,5,8]{4,2,3,1,0:T(8,128)} fusion(pred[8,5]{0,1:T(8,128)(4,1)S(1)} %copy-done.7, bf16[4,64,2,1,7,2]{4,0,5,2,1,3:T(4,128)(2,1)S(1)} %slice.28, bf16[4,64,2,1,8,5]{4,0,5,2,1,3:T(4,128)(2,1)S(1)} %copy.218, bf16[3,3,3,8,4]{3,4,2,1,0:T(4,128)(2,1)S(1)} %copy-done.6), kind=kOutput, calls=%fused_computation.19 | convolution fusion | flops 6049792 | bytes 220904 | tf_op jit(solution)/shard_map/conv_general_dilated | solution.py:135
  242.5 2.6 copy.219
  246.4 5.5 all-to-all-start.1
  253.0 8.2 %all-to-all-done.1 = f32[64,1,512]{2,1,0:T(1,128)S(1)} async-done(((f32[64,1,512]{2,1,0:T(1,128)}), f32[64,1,512]{2,1,0:T(1,128)S(1)}, u32[]{:S(2)}, u32[]{:S(2)}) %all-to-all-start.1) | async-done | bytes 131104 | tf_op jit(solution)/shard_map/all_to_all | solution.py:144
  263.6 1.3 fusion.51
  264.9 73.3 %all-reduce.4 = (f32[256]{0:T(256)S(1)}, f32[256]{0:T(256)S(1)}) all-reduce(f32[256]{0:T(256)S(1)} %get-tuple-element.252, f32[256]{0:T(256)S(1)} %get-tuple-element.251), channel_id=1, replica_groups=mesh['dp'=4,'space'=64] {'dp','space'}, use_global_device_ids=true, to_apply=%region_16.17 | all-reduce | flops 512 | bytes 4096 | tf_op jit(solution)/shard_map/psum | solution.py:151
  339.4 2.8 fusion.53
  344.1 3.5 copy.231
  348.3 3.4 copy.230
  351.7 29.6 %fusion.54 = f32[3,3,3,8,4]{3,4,2,1,0:T(4,128)S(1)} fusion(bf16[1,8,64,2,32]{1,0,4,3,2:T(2,128)(2,1)} %copy.230, bf16[1,4,64,2,32]{1,0,4,3,2:T(2,128)(2,1)} %copy.231), kind=kOutput, calls=%fused_computation.97 | convolution fusion | flops 4572160 | bytes 101760 | tf_op jit(solution)/shard_map/vmap()/conv_general_dilated | solution.py:42
  381.3 151.0 %all-reduce.10.cloned.1.call-done = f32[3,3,3,128,256]{3,4,2,1,0:T(8,128)} async-done(((f32[3,3,3,128,256]{3,4,2,1,0:T(8,128)}), f32[3,3,3,128,256]{3,4,2,1,0:T(8,128)}) %all-reduce.10.cloned.1.call-update) | async-done | bytes 3538960
  533.3 18.7 %all-reduce.5 = (f32[3,3,3,128,4]{3,4,2,1,0:T(4,128)}, f32[3,3,3,8,4]{3,4,2,1,0:T(4,128)}) all-reduce(f32[3,3,3,128,4]{3,4,2,1,0:T(4,128)S(1)} %constant_dynamic-slice_fusion.3, f32[3,3,3,8,4]{3,4,2,1,0:T(4,128)S(1)} %fusion.54), channel_id=1, replica_groups=mesh['dp'=4,'space'=64] {'dp'}, use_global_device_ids=true, to_apply=%region_17.18 | all-reduce | flops 14688 | bytes 117504 | tf_op jit(solution)/shard_map/psum | solution.py:167
  (115 shorter events, 23.4 us)
Async XLA Ops:
  7.2 13.3 %copy-start = (bf16[3,3,3,128,256]{4,3,2,1,0:T(8,128)(2,1)S(1)}, bf16[3,3,3,128,256]{4,3,2,1,0:T(8,128)(2,1)}, u32[]{:S(2)}) copy-start(bf16[3,3,3,128,256]{4,3,2,1,0:T(8,128)(2,1)} %param.11) | copy-start | bytes 5308420
  7.2 13.3 %copy-start.7 = (pred[8,5]{0,1:T(8,128)(4,1)S(1)}, pred[8,5]{0,1:T(8,128)(4,1)}, u32[]{:S(2)}) copy-start(pred[8,5]{0,1:T(8,128)(4,1)} %constant.99) | copy-start | bytes 124
  8.3 9.8 %collective-permute-start = (bf16[1,1,4,64,128]{4,0,3,2,1:T(2,128)(2,1)S(1)}, bf16[1,1,4,64,128]{4,0,3,2,1:T(2,128)(2,1)S(1)}, u32[]{:S(2)}, u32[]{:S(2)}) collective-permute-start(bf16[1,1,4,64,128]{4,0,3,2,1:T(2,128)(2,1)S(1)} %copy.254), channel_id=1, source_target_pairs={{0,1},{1,2},{2,3},{3,4},{4,5},{5,6},{6,7},{7,8},{8,9},{9,10},{10,1... | collective-permute-start | bytes 196616 | tf_op jit(solution)/shard_map/ppermute | solution.py:15
  19.4 0.7 copy-start.1
  20.1 150.2 %copy-start.8 = (f32[256]{0:T(256)S(1)}, f32[256]{0:T(256)}, u32[]{:S(2)}) copy-start(f32[256]{0:T(256)} %param.12) | copy-start | bytes 3076
  20.1 150.2 %copy-start.11 = (f32[256]{0:T(256)S(1)}, f32[256]{0:T(256)}, u32[]{:S(2)}) copy-start(f32[256]{0:T(256)} %param.13) | copy-start | bytes 3076
  20.5 159.8 %copy-start.5 = (bf16[3,3,3,8,4]{3,4,2,1,0:T(4,128)(2,1)S(1)}, bf16[3,3,3,8,4]{3,4,2,1,0:T(4,128)(2,1)}, u32[]{:S(2)}) copy-start(bf16[3,3,3,8,4]{3,4,2,1,0:T(4,128)(2,1)} %param.14) | copy-start | bytes 5188
  20.5 160.4 %copy-start.14 = (u32[256]{0:T(256)S(1)}, u32[256]{0:T(256)}, u32[]{:S(2)}) copy-start(u32[256]{0:T(256)} %constant.108) | copy-start | bytes 3076
  170.3 0.6 copy-start.9
  172.2 16.9 %all-to-all-start = ((bf16[64,2,256]{2,1,0:T(2,128)(2,1)}), bf16[64,2,256]{2,1,0:T(2,128)(2,1)S(1)}, u32[]{:S(2)}, u32[]{:S(2)}) async-start(bf16[64,2,256]{2,1,0:T(2,128)(2,1)} %reshape.180), calls=%async_computation | async-start | bytes 131072 | tf_op jit(solution)/shard_map/all_to_all | solution.py:86
  198.1 26.0 %copy-start.10 = (f32[4]{0:T(128)S(1)}, f32[4]{0:T(128)}, u32[]{:S(2)}) copy-start(f32[4]{0:T(128)} %param.15) | copy-start | bytes 52
  198.1 26.1 %copy-start.12 = (f32[4]{0:T(128)S(1)}, f32[4]{0:T(128)}, u32[]{:S(2)}) copy-start(f32[4]{0:T(128)} %param.16) | copy-start | bytes 52
  198.1 26.9 %copy-start.4 = (bf16[1,4,64,2,32]{2,4,3,1,0:T(8,128)(2,1)S(1)}, bf16[1,4,64,2,32]{2,4,3,1,0:T(8,128)(2,1)}, u32[]{:S(2)}) copy-start(bf16[1,4,64,2,32]{2,4,3,1,0:T(8,128)(2,1)} %param.17) | copy-start | bytes 98308
  199.8 35.7 %copy-start.6 = (bf16[3,3,3,8,4]{3,4,2,1,0:T(4,128)(2,1)S(1)}, bf16[3,3,3,8,4]{3,4,2,1,0:T(4,128)(2,1)}, u32[]{:S(2)}) copy-start(bf16[3,3,3,8,4]{3,4,2,1,0:T(4,128)(2,1)} %rev.3) | copy-start | bytes 5188
  246.4 14.9 %all-to-all-start.1 = ((f32[64,1,512]{2,1,0:T(1,128)}), f32[64,1,512]{2,1,0:T(1,128)S(1)}, u32[]{:S(2)}, u32[]{:S(2)}) async-start(f32[64,1,512]{2,1,0:T(1,128)} %reshape.182), calls=%async_computation.1 | async-start | bytes 262144 | tf_op jit(solution)/shard_map/all_to_all | solution.py:144
  251.8 280.5 %all-reduce.10.cloned.1.call-start = ((), (), s32[]{:S(2)}) async-start(), calls=%async_computation.2 | async-start | bytes 7077888
  262.7 76.7 %copy-start.2 = (bf16[1,3,4,64,128]{4,0,3,2,1:T(2,128)(2,1)S(1)}, bf16[1,3,4,64,128]{4,0,3,2,1:T(2,128)(2,1)}, u32[]{:S(2)}) copy-start(bf16[1,3,4,64,128]{4,0,3,2,1:T(2,128)(2,1)} %copy-done.1) | copy-start | bytes 589828
  342.2 0.7 copy-start.13
  342.2 5.4 copy-start.3
Sparse Core Ops, SparseCore 0:
  342.4 189.9 all-reduce.9
where the time goes:
time: 568 us; the launch traced here: 559 us
  blocking collectives  259 us (46%)
  waiting for transfers between devices  173 us (30%)
  matrix products  45.4 us (8%)
  local copies, waits for them, and re-layouts  31 us (5%)
  between operations  16.8 us (3%)
  starting transfers between devices  15.5 us (3%)
  loops' own time  11.6 us (2%)
  other arithmetic  6.47 us (1%)
    unnamed x2, waiting for transfers between devices  151 us
    psum x1, blocking collectives, per_device(): lax.psum(jnp.sum(pre_one, axis=axes_last), ('dp', 'space')) / count  74.9 us
    psum x1, blocking collectives, per_device(): lax.psum(jnp.sum(jnp.square(pre_one - mean_one), axis=axes_last), ('dp',...  74.4 us
    psum x1, blocking collectives, per_device(): lax.psum((jnp.sum(grad_norm_one, axis=axes_last), jnp.sum(grad_norm_one *...  73.3 us
    conv_general_dilated x1, matrix products, group_filter(): lax.conv_general_dilated(inputs, grads, (1, 1, 1), ((1, 1), (1, 1), (1, 1...  29.6 us
    psum x1, blocking collectives, per_device(): summed = lax.psum(local_one, 'dp')  18.7 us
    another operation x1, loops' own time, combined_all(): lax.fori_loop(1, lax.axis_size(axis), lambda source, state: combine(state...  11.6 us
  transfers between devices with their start and end apart: 4, of which 4 were waited for; matrix products, arithmetic and copies ran while one was open for 7% of the time, Pallas kernels for 0%

commit v1 on v0

--- a/solution.py
+++ b/solution.py
@@ -141,7 +141,10 @@
         feature_group_count=groups_here,
         preferred_element_type=jnp.float32,
     )
-    arrived = lax.all_to_all(partial_grad, "space", split_axis=2, concat_axis=1, tiled=True)
+    size = lax.axis_size("space")
+    blocks = jnp.stack(jnp.split(partial_grad, size, axis=2), axis=0)
+    blocks = lax.all_to_all(blocks, "space", split_axis=0, concat_axis=0)
+    arrived = jnp.concatenate(blocks, axis=1)
     grad_act = jnp.sum(
         arrived.reshape((lead, channels // window, replicas, window) + arrived.shape[2:]), axis=2
     ).reshape((lead, channels) + arrived.shape[2:])

time: 568 us -> 665 us (1.17)
  local copies, waits for them, and re-layouts: 31 us -> 125 us
    conv_general_dilated x5 -> x134, local copies, waits for them, and re-layouts: 3.54 us -> 78.9 us  [per_device(): lax.conv_general_dilated(grad_pre_two, turned, (1, 1, 1), padding_one, di...]
    unnamed x51 -> x198, local copies, waits for them, and re-layouts: 9.49 us -> 28.3 us
  transfers between devices with their start and end apart: 4 -> 4, of which waited for: 4 -> 4; matrix products, arithmetic and copies ran while one was open for 7% -> 6% of each run, Pallas kernels for 0% -> 0%
where the time goes in v1:
time: 665 us; the launch traced here: 653 us
  blocking collectives  259 us (39%)
  waiting for transfers between devices  174 us (26%)
  local copies, waits for them, and re-layouts  125 us (19%)
  matrix products  43.9 us (7%)
  between operations  17.7 us (3%)
  starting transfers between devices  15.5 us (2%)
  loops' own time  11.3 us (2%)
  other arithmetic  6.98 us (1%)
    unnamed x2, waiting for transfers between devices  151 us
    conv_general_dilated x134, local copies, waits for them, and re-layouts, per_device(): lax.conv_general_dilated(grad_pre_two, turned, (1, 1, 1), padding_one, di...  78.9 us
    psum x1, blocking collectives, per_device(): lax.psum(jnp.sum(pre_one, axis=axes_last), ('dp', 'space')) / count  74.9 us
    psum x1, blocking collectives, per_device(): lax.psum(jnp.sum(jnp.square(pre_one - mean_one), axis=axes_last), ('dp',...  74.4 us
    psum x1, blocking collectives, per_device(): lax.psum((jnp.sum(grad_norm_one, axis=axes_last), jnp.sum(grad_norm_one *...  73.3 us
    conv_general_dilated x1, matrix products, group_filter(): lax.conv_general_dilated(inputs, grads, (1, 1, 1), ((1, 1), (1, 1), (1, 1...  29.6 us
    unnamed x198, local copies, waits for them, and re-layouts  28.3 us
    psum x1, blocking collectives, per_device(): summed = lax.psum(local_one, 'dp')  18.7 us
  transfers between devices with their start and end apart: 4, of which 4 were waited for; matrix products, arithmetic and copies ran while one was open for 6% of the time, Pallas kernels for 0%

profile of v1, /device:TPU:2, one launch (start us, length us, event | category | flops | bytes accessed | tf_op | source)
XLA Modules:
  0.0 653.4 jit_solution(11982604458277611306)
XLA Ops:
  8.3 1.9 collective-permute-start
  10.2 7.9 %collective-permute-done = bf16[1,1,4,64,128]{4,0,3,2,1:T(2,128)(2,1)S(1)} collective-permute-done((bf16[1,1,4,64,128]{4,0,3,2,1:T(2,128)(2,1)S(1)}, bf16[1,1,4,64,128]{4,0,3,2,1:T(2,128)(2,1)S(1)}, u32[]{:S(2)}, u32[]{:S(2)}) %collective-permute-start) | collective-permute-done | bytes 65568 | tf_op jit(solution)/shard_map/ppermute | solution.py:15
  21.0 74.9 %psum.56 = f32[256]{0:T(256)S(1)} all-reduce(f32[256]{0:T(256)S(1)} %get-tuple-element.333), channel_id=1, replica_groups=mesh['dp'=4,'space'=64] {'dp','space'}, use_global_device_ids=true, to_apply=%region_1.0 | all-reduce | flops 256 | bytes 2048 | tf_op jit(solution)/shard_map/psum | solution.py:69
  96.0 74.4 %psum.57 = f32[256]{0:T(256)S(1)} all-reduce(f32[256]{0:T(256)S(1)} %select_reduce_fusion.2), channel_id=1, replica_groups=mesh['dp'=4,'space'=64] {'dp','space'}, use_global_device_ids=true, to_apply=%region_3.0 | all-reduce | flops 256 | bytes 2048 | tf_op jit(solution)/shard_map/psum | solution.py:70
  172.0 8.1 %all-to-all-start = ((bf16[64,2,256]{2,1,0:T(2,128)(2,1)}), bf16[64,2,256]{2,1,0:T(2,128)(2,1)S(1)}, u32[]{:S(2)}, u32[]{:S(2)}) async-start(bf16[64,2,256]{2,1,0:T(2,128)(2,1)} %reshape.364), calls=%async_computation | async-start | bytes 131072 | tf_op jit(solution)/shard_map/all_to_all | solution.py:86
  182.7 6.1 all-to-all-done
  190.0 2.1 copy.511
  192.3 5.6 fusion.8
  197.9 1.7 copy.512
  200.4 8.6 %all-reduce.7 = (f32[4]{0:T(128)S(1)}, f32[16]{0:T(128)S(1)}, f32[16]{0:T(128)S(1)}) all-reduce(f32[4]{0:T(128)S(1)} %dynamic-update-slice, f32[16]{0:T(128)S(1)} %get-tuple-element.332, f32[16]{0:T(128)S(1)} %dynamic-update-slice.2), channel_id=1, replica_groups=mesh['dp'=4,'space'=64] {'dp'}, use_global_device_ids=true, to_apply=%add | all-reduce | flops 36 | bytes 288
  209.6 13.3 %while.19 = (s32[]{:T(128)}, f32[1,1,1,1,1]{4,3,2,1,0:T(1,128)}, f32[1,4,1,1,1]{1,4,3,2,0:T(1,128)S(1)}, f32[1,4,1,1,1]{1,4,3,2,0:T(1,128)S(1)}, f32[4,1,1,1,1,1...) while((s32[]{:T(128)}, f32[1,1,1,1,1]{4,3,2,1,0:T(1,128)}, ...), condition=%wide.region_7.8_spmd, body=%wide.region_6.7_spmd.sunk | while | flops 37 | bytes 303 | solution.py:24
  224.7 9.1 %all-reduce.6 = (f32[1,4,1,1,1]{1,4,3,2,0:T(1,128)S(1)}, f32[1,4,1,1,1]{1,4,3,2,0:T(1,128)S(1)}) all-reduce(f32[1,4,1,1,1]{1,4,3,2,0:T(1,128)S(1)} %bitcast.935, f32[1,4,1,1,1]{1,4,3,2,0:T(1,128)S(1)} %bitcast.934), channel_id=1, replica_groups=mesh['dp'=4,'space'=64] {'dp'}, use_global_device_ids=true, to_apply=%region_11.12 | all-reduce | flops 8 | bytes 64 | tf_op jit(solution)/shard_map/psum | solution.py:114
  235.4 5.5 convolution_select_fusion
  326.6 12.5 %reshape.366 = f32[64,1,512]{2,1,0:T(1,128)} reshape(f32[64,1,1,2,8,32]{5,4,3,2,1,0:T(8,128)S(1)} %bitcast.858) | data formatting | bytes 262144
  339.2 5.5 all-to-all-start.1
  345.1 8.9 %all-to-all-done.1 = f32[64,1,512]{2,1,0:T(1,128)S(1)} async-done(((f32[64,1,512]{2,1,0:T(1,128)}), f32[64,1,512]{2,1,0:T(1,128)S(1)}, u32[]{:S(2)}, u32[]{:S(2)}) %all-to-all-start.1) | async-done | bytes 131104 | tf_op jit(solution)/shard_map/all_to_all | solution.py:146
  354.6 1.6 reduce.1
  359.3 73.3 %all-reduce.4 = (f32[256]{0:T(256)S(1)}, f32[256]{0:T(256)S(1)}) all-reduce(f32[256]{0:T(256)S(1)} %get-tuple-element.232, f32[256]{0:T(256)S(1)} %get-tuple-element.231), channel_id=1, replica_groups=mesh['dp'=4,'space'=64] {'dp','space'}, use_global_device_ids=true, to_apply=%region_16.17 | all-reduce | flops 512 | bytes 4096 | tf_op jit(solution)/shard_map/psum | solution.py:154
  433.7 2.8 fusion.57
  438.4 3.5 copy.660
  442.6 3.2 copy.659
  445.8 29.6 %fusion.58 = f32[3,3,3,8,4]{3,4,2,1,0:T(4,128)S(1)} fusion(bf16[1,8,64,2,32]{1,0,4,3,2:T(2,128)(2,1)} %copy.659, bf16[1,4,64,2,32]{1,0,4,3,2:T(2,128)(2,1)} %copy.660), kind=kOutput, calls=%fused_computation.228 | convolution fusion | flops 4572160 | bytes 101760 | tf_op jit(solution)/shard_map/vmap()/conv_general_dilated | solution.py:42
  475.4 151.1 %all-reduce.10.cloned.1.call-done = f32[3,3,3,128,256]{3,4,2,1,0:T(8,128)} async-done(((f32[3,3,3,128,256]{3,4,2,1,0:T(8,128)}), f32[3,3,3,128,256]{3,4,2,1,0:T(8,128)}) %all-reduce.10.cloned.1.call-update) | async-done | bytes 3538960
  627.5 18.7 %all-reduce.5 = (f32[3,3,3,128,4]{3,4,2,1,0:T(4,128)}, f32[3,3,3,8,4]{3,4,2,1,0:T(4,128)}) all-reduce(f32[3,3,3,128,4]{3,4,2,1,0:T(4,128)S(1)} %constant_dynamic-slice_fusion.3, f32[3,3,3,8,4]{3,4,2,1,0:T(4,128)S(1)} %fusion.58), channel_id=1, replica_groups=mesh['dp'=4,'space'=64] {'dp'}, use_global_device_ids=true, to_apply=%region_17.18 | all-reduce | flops 14688 | bytes 117504 | tf_op jit(solution)/shard_map/psum | solution.py:170
  (392 shorter events, 107.8 us)
Async XLA Ops:
  7.2 13.3 %copy-start = (bf16[3,3,3,128,256]{4,3,2,1,0:T(8,128)(2,1)S(1)}, bf16[3,3,3,128,256]{4,3,2,1,0:T(8,128)(2,1)}, u32[]{:S(2)}) copy-start(bf16[3,3,3,128,256]{4,3,2,1,0:T(8,128)(2,1)} %param.11) | copy-start | bytes 5308420
  8.3 9.8 %collective-permute-start = (bf16[1,1,4,64,128]{4,0,3,2,1:T(2,128)(2,1)S(1)}, bf16[1,1,4,64,128]{4,0,3,2,1:T(2,128)(2,1)S(1)}, u32[]{:S(2)}, u32[]{:S(2)}) collective-permute-start(bf16[1,1,4,64,128]{4,0,3,2,1:T(2,128)(2,1)S(1)} %copy.683), channel_id=1, source_target_pairs={{0,1},{1,2},{2,3},{3,4},{4,5},{5,6},{6,7},{7,8},{8,9},{9,10},{10,1... | collective-permute-start | bytes 196616 | tf_op jit(solution)/shard_map/ppermute | solution.py:15
  20.1 150.2 %copy-start.50 = (f32[256]{0:T(256)S(1)}, f32[256]{0:T(256)}, u32[]{:S(2)}) copy-start(f32[256]{0:T(256)} %param.12) | copy-start | bytes 3076
  20.1 150.2 %copy-start.53 = (f32[256]{0:T(256)S(1)}, f32[256]{0:T(256)}, u32[]{:S(2)}) copy-start(f32[256]{0:T(256)} %param.13) | copy-start | bytes 3076
  20.5 159.5 %copy-start.47 = (bf16[3,3,3,8,4]{3,4,2,1,0:T(4,128)(2,1)S(1)}, bf16[3,3,3,8,4]{3,4,2,1,0:T(4,128)(2,1)}, u32[]{:S(2)}) copy-start(bf16[3,3,3,8,4]{3,4,2,1,0:T(4,128)(2,1)} %param.14) | copy-start | bytes 5188
  20.5 160.2 %copy-start.56 = (u32[256]{0:T(256)S(1)}, u32[256]{0:T(256)}, u32[]{:S(2)}) copy-start(u32[256]{0:T(256)} %constant.108) | copy-start | bytes 3076
  172.0 16.9 %all-to-all-start = ((bf16[64,2,256]{2,1,0:T(2,128)(2,1)}), bf16[64,2,256]{2,1,0:T(2,128)(2,1)S(1)}, u32[]{:S(2)}, u32[]{:S(2)}) async-start(bf16[64,2,256]{2,1,0:T(2,128)(2,1)} %reshape.364), calls=%async_computation | async-start | bytes 131072 | tf_op jit(solution)/shard_map/all_to_all | solution.py:86
  197.9 25.7 %copy-start.52 = (f32[4]{0:T(128)S(1)}, f32[4]{0:T(128)}, u32[]{:S(2)}) copy-start(f32[4]{0:T(128)} %param.15) | copy-start | bytes 52
  197.9 25.7 %copy-start.54 = (f32[4]{0:T(128)S(1)}, f32[4]{0:T(128)}, u32[]{:S(2)}) copy-start(f32[4]{0:T(128)} %param.16) | copy-start | bytes 52
  197.9 26.5 %copy-start.6 = (bf16[1,4,64,2,32]{2,4,3,1,0:T(8,128)(2,1)S(1)}, bf16[1,4,64,2,32]{2,4,3,1,0:T(8,128)(2,1)}, u32[]{:S(2)}) copy-start(bf16[1,4,64,2,32]{2,4,3,1,0:T(8,128)(2,1)} %param.17) | copy-start | bytes 98308
  199.6 35.7 %copy-start.48 = (bf16[3,3,3,8,4]{3,4,2,1,0:T(4,128)(2,1)S(1)}, bf16[3,3,3,8,4]{3,4,2,1,0:T(4,128)(2,1)}, u32[]{:S(2)}) copy-start(bf16[3,3,3,8,4]{3,4,2,1,0:T(4,128)(2,1)} %rev.3) | copy-start | bytes 5188
  310.0 13.3 %copy-start.8 = (f32[1,2,1,40,8]{3,4,1,2,0:T(8,128)S(1)}, f32[1,2,1,40,8]{3,4,1,2,0:T(8,128)}, u32[]{:S(2)}) copy-start(f32[1,2,1,40,8]{3,4,1,2,0:T(8,128)} %reshape.167) | copy-start | bytes 7684
  310.0 16.6 %copy-start.11 = (f32[1,2,1,40,8]{3,4,1,2,0:T(8,128)S(1)}, f32[1,2,1,40,8]{3,4,1,2,0:T(8,128)}, u32[]{:S(2)}) copy-start(f32[1,2,1,40,8]{3,4,1,2,0:T(8,128)} %reshape.231) | copy-start | bytes 7684
  310.0 16.6 %copy-start.9 = (f32[1,2,1,40,8]{3,4,1,2,0:T(8,128)S(1)}, f32[1,2,1,40,8]{3,4,1,2,0:T(8,128)}, u32[]{:S(2)}) copy-start(f32[1,2,1,40,8]{3,4,1,2,0:T(8,128)} %reshape.233) | copy-start | bytes 7684
  310.7 15.9 %copy-start.7 = (f32[1,2,1,40,8]{3,4,1,2,0:T(8,128)S(1)}, f32[1,2,1,40,8]{3,4,1,2,0:T(8,128)}, u32[]{:S(2)}) copy-start(f32[1,2,1,40,8]{3,4,1,2,0:T(8,128)} %reshape.235) | copy-start | bytes 7684
  310.8 15.4 %copy-start.16 = (f32[1,2,1,40,8]{3,4,1,2,0:T(8,128)S(1)}, f32[1,2,1,40,8]{3,4,1,2,0:T(8,128)}, u32[]{:S(2)}) copy-start(f32[1,2,1,40,8]{3,4,1,2,0:T(8,128)} %reshape.205) | copy-start | bytes 7684
  310.8 15.7 %copy-start.15 = (f32[1,2,1,40,8]{3,4,1,2,0:T(8,128)S(1)}, f32[1,2,1,40,8]{3,4,1,2,0:T(8,128)}, u32[]{:S(2)}) copy-start(f32[1,2,1,40,8]{3,4,1,2,0:T(8,128)} %reshape.227) | copy-start | bytes 7684
  310.8 15.7 %copy-start.13 = (f32[1,2,1,40,8]{3,4,1,2,0:T(8,128)S(1)}, f32[1,2,1,40,8]{3,4,1,2,0:T(8,128)}, u32[]{:S(2)}) copy-start(f32[1,2,1,40,8]{3,4,1,2,0:T(8,128)} %reshape.229) | copy-start | bytes 7684
  311.7 14.8 %copy-start.19 = (f32[1,2,1,40,8]{3,4,1,2,0:T(8,128)S(1)}, f32[1,2,1,40,8]{3,4,1,2,0:T(8,128)}, u32[]{:S(2)}) copy-start(f32[1,2,1,40,8]{3,4,1,2,0:T(8,128)} %reshape.225) | copy-start | bytes 7684
  312.6 13.9 %copy-start.25 = (f32[1,2,1,40,8]{3,4,1,2,0:T(8,128)S(1)}, f32[1,2,1,40,8]{3,4,1,2,0:T(8,128)}, u32[]{:S(2)}) copy-start(f32[1,2,1,40,8]{3,4,1,2,0:T(8,128)} %reshape.221) | copy-start | bytes 7684
  312.6 13.9 %copy-start.22 = (f32[1,2,1,40,8]{3,4,1,2,0:T(8,128)S(1)}, f32[1,2,1,40,8]{3,4,1,2,0:T(8,128)}, u32[]{:S(2)}) copy-start(f32[1,2,1,40,8]{3,4,1,2,0:T(8,128)} %reshape.223) | copy-start | bytes 7684
  339.2 14.9 %all-to-all-start.1 = ((f32[64,1,512]{2,1,0:T(1,128)}), f32[64,1,512]{2,1,0:T(1,128)S(1)}, u32[]{:S(2)}, u32[]{:S(2)}) async-start(f32[64,1,512]{2,1,0:T(1,128)} %reshape.366), calls=%async_computation.1 | async-start | bytes 262144 | tf_op jit(solution)/shard_map/all_to_all | solution.py:146
  344.7 281.9 %all-reduce.10.cloned.1.call-start = ((), (), s32[]{:S(2)}) async-start(), calls=%async_computation.2 | async-start | bytes 7077888
  356.2 77.5 %copy-start.2 = (bf16[1,3,4,64,128]{4,0,3,2,1:T(2,128)(2,1)S(1)}, bf16[1,3,4,64,128]{4,0,3,2,1:T(2,128)(2,1)}, u32[]{:S(2)}) copy-start(bf16[1,3,4,64,128]{4,0,3,2,1:T(2,128)(2,1)} %copy-done.1) | copy-start | bytes 589828
  (37 other events, 318.4 us)
Sparse Core Ops, SparseCore 0:
  436.7 189.8 all-reduce.9
